TPU v7x, 512 devices: a whole 4x4x16 slice. The times are simulated.
512 devices in a mesh: gz: 32 (over y, z_hi, core), gy: 16 (over z_lo, x).
Axes of the slice: x: 4, y: 4, z: 16 (z_hi: 4, z_lo: 4; z = z_hi * 4 + z_lo), core: 2. Of those that a mesh axis runs over, the one named last changes fastest.
Arguments:
- features: bfloat16 [16, 128, 128, 128], P(None, 'gz', 'gy'), may hold values from -6 to 6
- labels: int32 [128, 128, 128], P('gz', 'gy'), may hold values from 0 to 1
- sign_map: int32 [128, 128, 128], P('gz', 'gy'), may hold values from 0 to 1
- conv_first: bfloat16 [16, 16, 3, 3, 3], replicated, may hold values from -0.3125 to 0.3125
- conv_second: bfloat16 [16, 16, 3, 3, 3], replicated, may hold values from -0.3125 to 0.3125
- speed_weight: float32 [16], replicated, may hold values from -1.5 to 1.5
Outputs:
- d_features: bfloat16 [16, 128, 128, 128], P(None, 'gz', 'gy')
- grad_first: float32 [16, 16, 3, 3, 3], replicated
- grad_second: float32 [16, 16, 3, 3, 3], replicated
- grad_speed: float32 [16], replicated
All inputs are finite; a program needn't handle non-finite values.
Results may differ from a plain program's by a relative error of at most 0.01.
Values may be sent and summed in bfloat16 or wider, within the bound.
No kernel may reach another device: no remote copies, remote signals or barrier semaphores. Data moves between devices by JAX's collectives and lax.ppermute only.
A program may use at most 128 MiB of HBM per device.

v0:
```python
import jax
import jax.numpy as jnp
from jax import lax
from jax.sharding import PartitionSpec as P

C = 16
STEPS = 4
time_step = 0.25
spread_rate = 0.5
slope_floor = 0.1
layout = ("NCDHW", "OIDHW", "NCDHW")


def extended(value, sides, width):
    for axis, dim in sides:
        size, length = (lax.axis_size(axis), value.shape[dim])
        up = [(i, (i + 1) % size) for i in range(size - 1)]
        down = [(j, i) for i, j in up]
        last = lax.slice_in_dim(value, length - width, length, axis=dim)
        initial = lax.slice_in_dim(value, 0, width, axis=dim)
        before = lax.ppermute(last, axis, up)
        after = lax.ppermute(initial, axis, down)
        value = jnp.concatenate([before, value, after], axis=dim)
    return value


def for_sending(value):
    return jax.tree.map(lambda a: a.astype(jnp.bfloat16) if a.dtype == jnp.float32 else a, value)


def from_behind(block, axis, distance):
    devices = range(lax.axis_size(axis))
    route = [(i - distance, i) for i in devices if i - distance in devices]
    return lax.ppermute(block, axis, route)


def front(padded, speed):
    grid = jnp.pad(padded, ((0, 0), (0, 0), (1, 1)))
    centre = grid[1:-1, 1:-1, 1:-1]
    up_z = grid[2:, 1:-1, 1:-1]
    low_z = grid[:-2, 1:-1, 1:-1]
    up_y = grid[1:-1, 2:, 1:-1]
    low_y = grid[1:-1, :-2, 1:-1]
    up_x = grid[1:-1, 1:-1, 2:]
    low_x = grid[1:-1, 1:-1, :-2]
    dif_z = (up_z - low_z) * 0.5
    dif_y = (up_y - low_y) * 0.5
    dif_x = (up_x - low_x) * 0.5
    slope = jnp.sqrt(dif_z * dif_z + dif_y * dif_y + dif_x * dif_x + slope_floor)
    laplace = up_z + low_z + up_y + low_y + up_x + low_x - 6.0 * centre
    return centre + time_step * (speed * slope + spread_rate * laplace)


def silu_slope(value):
    sig = jax.nn.sigmoid(value)
    return sig * (1.0 + value * (1.0 - sig))


def conv_halo(field):
    return extended(field, (("gz", 1), ("gy", 2)), 1)


def conv_local(padded, weight):
    grid = jnp.pad(padded, ((0, 0), (0, 0), (0, 0), (1, 1)))
    return lax.conv_general_dilated(
        grid[None],
        weight,
        (1, 1, 1),
        "VALID",
        dimension_numbers=layout,
        preferred_element_type=jnp.float32,
    )[0]


def flip_weight(weight):
    return jnp.flip(weight, (2, 3, 4)).transpose(1, 0, 2, 3, 4)


def weight_grad(padded, d_out):
    grid = jnp.pad(padded, ((0, 0), (0, 0), (0, 0), (1, 1)))
    d_weight = lax.conv_general_dilated(
        grid[:, None],
        d_out[:, None],
        (1, 1, 1),
        "VALID",
        dimension_numbers=layout,
        preferred_element_type=jnp.float32,
    )
    return d_weight.transpose(1, 0, 2, 3, 4)


def conv_back(weight, d_out):
    d_grid = lax.conv_general_dilated(
        d_out[None],
        flip_weight(weight),
        (1, 1, 1),
        ((2, 2), (2, 2), (2, 2)),
        dimension_numbers=layout,
        preferred_element_type=jnp.float32,
    )[0]
    return d_grid[..., 1:-1]


def fold_axis(grad, width, dim, which):
    inner = grad.shape[dim] - 2 * width
    lower = lax.slice_in_dim(grad, 0, width, axis=dim)
    upper = lax.slice_in_dim(grad, inner + width, inner + 2 * width, axis=dim)
    core = lax.slice_in_dim(grad, width, inner + width, axis=dim)
    if which == 0:
        from_below = from_behind(for_sending(upper), "gz", 1).astype(upper.dtype)
        from_above = from_behind(for_sending(lower), "gz", -1).astype(lower.dtype)
    else:
        from_below = from_behind(for_sending(upper), "gy", 1).astype(upper.dtype)
        from_above = from_behind(for_sending(lower), "gy", -1).astype(lower.dtype)
    head = [(0, 0)] * grad.ndim
    tail = [(0, 0)] * grad.ndim
    head[dim] = (0, inner - width)
    tail[dim] = (inner - width, 0)
    return core + jnp.pad(from_below, head) + jnp.pad(from_above, tail)


def fold_rims(grad, width, zdim):
    return fold_axis(fold_axis(grad, width, zdim, 0), width, zdim + 1, 1)


def input_grad(weight, d_out):
    return fold_rims(conv_back(weight, d_out), 1, 1)


def on_device(features, labels, sign_map, conv_first, conv_second, speed_weight):
    high = lax.Precision.HIGHEST
    feat_pad = conv_halo(features)
    act_first = conv_local(feat_pad, conv_first)
    hidden = jax.nn.silu(act_first).astype(jnp.bfloat16)
    hidden_pad = conv_halo(hidden)
    act_second = conv_local(hidden_pad, conv_second)
    top = jax.nn.silu(act_second)
    speed = jnp.tanh(jnp.einsum("c,czyx->zyx", speed_weight, top, precision=high))
    phi_start = 2.0 * sign_map.astype(jnp.float32) - 1.0
    target = labels.astype(jnp.float32)
    stored = []
    phi = phi_start
    for step in range(STEPS):
        padded = extended(phi, (("gz", 0), ("gy", 1)), 1)
        stored.append(padded)
        phi = front(padded, speed)
    d_phi = jax.nn.sigmoid(phi) - target
    d_speed = jnp.zeros_like(speed)
    for padded in reversed(stored):
        back = jax.vjp(front, padded, speed)[1]
        d_padded, d_part = back(d_phi)
        d_speed = d_speed + d_part
        d_phi = fold_rims(d_padded, 1, 0)
    d_pre = d_speed * (1.0 - speed * speed)
    raw_speed = jnp.einsum("zyx,czyx->c", d_pre, top, precision=high)
    d_second = (speed_weight[:, None, None, None] * d_pre[None] * silu_slope(act_second)).astype(
        jnp.bfloat16
    )
    raw_second = weight_grad(hidden_pad, d_second)
    d_hidden = input_grad(conv_second, d_second)
    d_first = (d_hidden * silu_slope(act_first)).astype(jnp.bfloat16)
    raw_first = weight_grad(feat_pad, d_first)
    d_feat = input_grad(conv_first, d_first)
    raw_first, raw_second, raw_speed = lax.psum((raw_first, raw_second, raw_speed), ("gz", "gy"))
    total = (
        jnp.sum(raw_first * raw_first)
        + jnp.sum(raw_second * raw_second)
        + jnp.sum(raw_speed * raw_speed)
    )
    count = 54.0 * C * C + C
    factor = 1.0 / jnp.maximum(jnp.sqrt(total) / jnp.sqrt(jnp.float32(count)), 1.0)
    return (
        d_feat.astype(jnp.bfloat16),
        raw_first * factor,
        raw_second * factor,
        raw_speed * factor,
    )


def solution(mesh):
    in_specs = (P(None, "gz", "gy", None), P("gz", "gy", None), P("gz", "gy", None), P(), P(), P())
    out_specs = (P(None, "gz", "gy", None), P(), P(), P())
    return jax.shard_map(
        on_device, mesh=mesh, in_specs=in_specs, out_specs=out_specs, check_vma=False
    )
```

profile of v0, /device:TPU:15, one launch (start us, length us, event | category | flops | bytes accessed | tf_op | source)
XLA Modules:
  0.0 515.8 jit_solution(8016700852686420210)
XLA Ops:
  1.5 9.4 %collective-permute-start = (bf16[16,1,8,128]{3,0,2,1:T(8,128)(2,1)S(1)}, bf16[16,1,8,128]{3,0,2,1:T(8,128)(2,1)S(1)}, u32[]{:S(2)}, u32[]{:S(2)}) collective-permute-start(bf16[16,1,8,128]{3,0,2,1:T(8,128)(2,1)S(1)} %copy.83), channel_id=1, source_target_pairs={{0,16},{16,32},{32,48},{48,64},{64,80},{80,96},{96,112},{112,128},... | collective-permute-start | bytes 98312 | tf_op jit(solution)/shard_map/ppermute | solution.py:21
  14.5 5.5 %collective-permute-done.1 = bf16[16,1,8,128]{3,0,2,1:T(8,128)(2,1)S(1)} collective-permute-done((bf16[16,1,8,128]{3,0,2,1:T(8,128)(2,1)S(1)}, bf16[16,1,8,128]{3,0,2,1:T(8,128)(2,1)S(1)}, u32[]{:S(2)}, u32[]{:S(2)}) %collective-permute-start.1) | collective-permute-done | bytes 32800 | tf_op jit(solution)/shard_map/ppermute | solution.py:22
  20.0 3.5 collective-permute-start.2
  27.4 7.5 %collective-permute-start.9 = (f32[1,8,128]{2,1,0:T(8,128)S(1)}, f32[1,8,128]{2,1,0:T(8,128)S(1)}, u32[]{:S(2)}, u32[]{:S(2)}) collective-permute-start(f32[1,8,128]{2,1,0:T(8,128)S(1)} %get-tuple-element.113), channel_id=1, source_target_pairs={{0,16},{16,32},{32,48},{48,64},{64,80},{80,96},{96,112},{112,128},... | collective-permute-start | bytes 12296 | tf_op jit(solution)/shard_map/ppermute | solution.py:21
  37.6 4.2 copy.46
  42.8 5.8 %fusion.6 = f32[4,8,8,17,16]{4,2,3,1,0:T(8,128)} fusion(bf16[16,16,3,3,3]{1,0,4,3,2:T(8,128)(2,1)S(1)} %copy-done.23, bf16[16,6,10,1,7,2]{0,4,5,2,1,3:T(8,128)(2,1)S(1)} %slice.441, bf16[16,6,10,1,8,17]{0,4,5,2,1,3:T(8,128)(2,1)} %copy.46), kind=kOutput, calls=%fused_computation.8 | convolution fusion | flops 61037568 | bytes 580352 | tf_op jit(solution)/shard_map/conv_general_dilated | solution.py:65
  53.3 3.5 collective-permute-start.4
  61.2 4.9 collective-permute-start.11
  66.2 4.4 collective-permute-start.6
  72.9 4.4 collective-permute-done.7
  79.9 4.2 copy.50
  85.1 5.8 %fusion.10 = f32[4,8,8,17,16]{4,2,3,1,0:T(8,128)} fusion(bf16[16,16,3,3,3]{1,0,4,3,2:T(8,128)(2,1)S(1)} %copy-done, bf16[16,6,10,1,7,2]{0,4,5,2,1,3:T(8,128)(2,1)S(1)} %slice.445, bf16[16,6,10,1,8,17]{0,4,5,2,1,3:T(8,128)(2,1)} %copy.50), kind=kOutput, calls=%fused_computation.11 | convolution fusion | flops 61037568 | bytes 580352 | tf_op jit(solution)/shard_map/conv_general_dilated | solution.py:65
  98.0 5.6 %collective-permute-start.12 = (f32[1,8,128]{2,1,0:T(8,128)S(1)}, f32[1,8,128]{2,1,0:T(8,128)S(1)}, u32[]{:S(2)}, u32[]{:S(2)}) collective-permute-start(f32[1,8,128]{2,1,0:T(8,128)S(1)} %get-tuple-element.112), channel_id=1, source_target_pairs={{16,0},{32,16},{48,32},{64,48},{80,64},{96,80},{112,96},{128,112},... | collective-permute-start | bytes 12296 | tf_op jit(solution)/shard_map/ppermute | solution.py:22
  103.5 4.3 collective-permute-start.13
  110.5 5.5 %collective-permute-start.15 = (f32[6,1,128]{2,1,0:T(1,128)S(1)}, f32[6,1,128]{2,1,0:T(1,128)S(1)}, u32[]{:S(2)}, u32[]{:S(2)}) collective-permute-start(f32[6,1,128]{2,1,0:T(1,128)S(1)} %get-tuple-element.96), channel_id=1, source_target_pairs={{0,1},{1,2},{2,3},{3,4},{4,5},{5,6},{6,7},{7,8},{8,9},{9,10},{10,1... | collective-permute-start | bytes 9224 | tf_op jit(solution)/shard_map/ppermute | solution.py:21
  116.9 8.6 %collective-permute-start.16 = (f32[1,8,128]{2,1,0:T(8,128)S(1)}, f32[1,8,128]{2,1,0:T(8,128)S(1)}, u32[]{:S(2)}, u32[]{:S(2)}) collective-permute-start(f32[1,8,128]{2,1,0:T(8,128)S(1)} %get-tuple-element.110), channel_id=1, source_target_pairs={{16,0},{32,16},{48,32},{64,48},{80,64},{96,80},{112,96},{128,112},... | collective-permute-start | bytes 12296 | tf_op jit(solution)/shard_map/ppermute | solution.py:22
  130.7 6.0 %collective-permute-start.19 = (f32[6,1,128]{2,1,0:T(1,128)S(1)}, f32[6,1,128]{2,1,0:T(1,128)S(1)}, u32[]{:S(2)}, u32[]{:S(2)}) collective-permute-start(f32[6,1,128]{2,1,0:T(1,128)S(1)} %get-tuple-element.94), channel_id=1, source_target_pairs={{0,1},{1,2},{2,3},{3,4},{4,5},{5,6},{6,7},{7,8},{8,9},{9,10},{10,1... | collective-permute-start | bytes 9224 | tf_op jit(solution)/shard_map/ppermute | solution.py:21
  137.7 9.2 %collective-permute-start.20 = (f32[1,8,128]{2,1,0:T(8,128)S(1)}, f32[1,8,128]{2,1,0:T(8,128)S(1)}, u32[]{:S(2)}, u32[]{:S(2)}) collective-permute-start(f32[1,8,128]{2,1,0:T(8,128)S(1)} %get-tuple-element.108), channel_id=1, source_target_pairs={{16,0},{32,16},{48,32},{64,48},{80,64},{96,80},{112,96},{128,112},... | collective-permute-start | bytes 12296 | tf_op jit(solution)/shard_map/ppermute | solution.py:22
  151.9 6.0 %collective-permute-start.23 = (f32[6,1,128]{2,1,0:T(1,128)S(1)}, f32[6,1,128]{2,1,0:T(1,128)S(1)}, u32[]{:S(2)}, u32[]{:S(2)}) collective-permute-start(f32[6,1,128]{2,1,0:T(1,128)S(1)} %get-tuple-element.92), channel_id=1, source_target_pairs={{0,1},{1,2},{2,3},{3,4},{4,5},{5,6},{6,7},{7,8},{8,9},{9,10},{10,1... | collective-permute-start | bytes 9224 | tf_op jit(solution)/shard_map/ppermute | solution.py:21
  159.8 8.5 %collective-permute-start.24 = (bf16[1,10,128]{2,1,0:T(8,128)(2,1)S(1)}, bf16[1,10,128]{2,1,0:T(8,128)(2,1)S(1)}, u32[]{:S(2)}, u32[]{:S(2)}) collective-permute-start(bf16[1,10,128]{2,1,0:T(8,128)(2,1)S(1)} %get-tuple-element.85), channel_id=1, source_target_pairs={{0,16},{16,32},{32,48},{48,64},{64,80},{80,96},{96,112},{112,128},... | collective-permute-start | bytes 7688 | tf_op jit(solution)/shard_map/ppermute | solution.py:34
  171.2 6.0 %collective-permute-done.25 = bf16[1,10,128]{2,1,0:T(8,128)(2,1)S(1)} collective-permute-done((bf16[1,10,128]{2,1,0:T(8,128)(2,1)S(1)}, bf16[1,10,128]{2,1,0:T(8,128)(2,1)S(1)}, u32[]{:S(2)}, u32[]{:S(2)}) %collective-permute-start.25) | collective-permute-done | bytes 2592 | tf_op jit(solution)/shard_map/ppermute | solution.py:34
  177.3 6.0 %collective-permute-start.26 = (bf16[4,1,128]{2,1,0:T(2,128)(2,1)S(1)}, bf16[4,1,128]{2,1,0:T(2,128)(2,1)S(1)}, u32[]{:S(2)}, u32[]{:S(2)}) collective-permute-start(bf16[4,1,128]{2,1,0:T(2,128)(2,1)S(1)} %get-tuple-element.104), channel_id=1, source_target_pairs={{0,1},{1,2},{2,3},{3,4},{4,5},{5,6},{6,7},{7,8},{8,9},{9,10},{10,1... | collective-permute-start | bytes 3080 | tf_op jit(solution)/shard_map/ppermute | solution.py:34
  185.3 4.5 collective-permute-done.27
  190.5 3.4 collective-permute-start.28
  193.9 3.7 collective-permute-start.29
  197.7 5.4 %collective-permute-done.29 = bf16[1,10,128]{2,1,0:T(8,128)(2,1)S(1)} collective-permute-done((bf16[1,10,128]{2,1,0:T(8,128)(2,1)S(1)}, bf16[1,10,128]{2,1,0:T(8,128)(2,1)S(1)}, u32[]{:S(2)}, u32[]{:S(2)}) %collective-permute-start.29) | collective-permute-done | bytes 2592 | tf_op jit(solution)/shard_map/ppermute | solution.py:34
  205.1 3.4 collective-permute-start.31
  208.5 3.0 collective-permute-done.31
  215.1 4.6 collective-permute-start.33
  219.8 4.2 collective-permute-done.33
  227.2 3.6 collective-permute-start.35
  230.8 6.7 %copy.62 = bf16[16,1,6,10,130]{0,1,4,3,2:T(2,128)(2,1)} copy(bf16[16,1,6,10,130]{4,0,3,2,1:T(8,128)(2,1)S(1)} %copy-done.4) | data formatting | bytes 499200 | tf_op jit(solution)/shard_map/broadcast_in_dim | solution.py:82
  237.6 6.7 %copy.64 = bf16[16,1,6,10,130]{0,1,4,3,2:T(2,128)(2,1)} copy(bf16[16,1,6,10,130]{4,0,3,2,1:T(8,128)(2,1)S(1)} %copy-done.5) | data formatting | bytes 499200 | tf_op jit(solution)/shard_map/broadcast_in_dim | solution.py:82
  249.2 3.8 copy.65
  257.6 8.0 %convolution_select_fusion.1 = f32[6,10,8,17,16]{4,2,3,1,0:T(8,128)} fusion(bf16[16,16,3,3,3]{1,0,4,3,2:T(8,128)(2,1)S(1)} %copy-done, pred[8,17]{0,1:T(8,128)(4,1)S(1)} %copy-done.25, bf16[16,4,8,1,7,2]{0,4,5,2,1,3:T(8,128)(2,1)S(1)} %slice.482, bf16[16,4,8,1,8,17]{0,4,5,2,1,3:T(8,128)(2,1)} %copy.56), kind=kOutput, calls=%fused_computation.19 | convolution fusion | flops 60759552 | bytes 689800 | tf_op jit(solution)/shard_map/conv_general_dilated | solution.py:93
  265.5 6.2 %copy.57 = f32[6,10,8,17,16]{3,2,4,1,0:T(8,128)} copy(f32[6,10,8,17,16]{4,2,3,1,0:T(8,128)} %convolution_select_fusion.1) | data formatting | bytes 1044480 | tf_op jit(solution)/shard_map/conv_general_dilated | solution.py:93
  271.8 3.2 reshape.79
  277.6 5.9 %collective-permute-start.37 = (bf16[16,1,10,128]{3,0,2,1:T(8,128)(2,1)S(1)}, bf16[16,1,10,128]{3,0,2,1:T(8,128)(2,1)S(1)}, u32[]{:S(2)}, u32[]{:S(2)}) collective-permute-start(bf16[16,1,10,128]{3,0,2,1:T(8,128)(2,1)S(1)} %get-tuple-element.52), channel_id=1, source_target_pairs={{16,0},{32,16},{48,32},{64,48},{80,64},{96,80},{112,96},{128,112},... | collective-permute-start | bytes 122888 | tf_op jit(solution)/shard_map/ppermute | solution.py:34
  283.6 29.5 %fusion.120 = f32[16,16,3,3,3]{0,1,4,3,2:T(8,128)S(1)} fusion(bf16[16,1,6,10,130]{0,1,4,3,2:T(2,128)(2,1)} %copy.64, bf16[16,1,4,8,128]{0,1,4,3,2:T(2,128)(2,1)} %copy.65), kind=kOutput, calls=%fused_computation.275 | convolution fusion | flops 56623104 | bytes 408320 | tf_op jit(solution)/shard_map/transpose | solution.py:89
  313.4 3.8 collective-permute-start.38
  319.5 4.3 collective-permute-done.39
  326.7 6.7 %convolution_select_fusion = f32[6,10,8,17,16]{4,2,3,1,0:T(8,128)} fusion(bf16[16,16,3,3,3]{1,0,4,3,2:T(8,128)(2,1)S(1)} %copy-done.24, pred[8,17]{0,1:T(8,128)(4,1)S(1)} %copy-done.25, bf16[16,4,8,1,7,2]{0,4,5,2,1,3:T(8,128)(2,1)S(1)} %slice.490, bf16[16,4,8,1,8,17]{0,4,5,2,1,3:T(8,128)(2,1)S(1)} %copy.60), kind=kOutput, calls=%fused_computation.18 | convolution fusion | flops 60759552 | bytes 689800 | tf_op jit(solution)/shard_map/conv_general_dilated | solution.py:93
  333.4 6.3 %copy.61 = f32[6,10,8,17,16]{3,2,4,1,0:T(8,128)} copy(f32[6,10,8,17,16]{4,2,3,1,0:T(8,128)} %convolution_select_fusion) | data formatting | bytes 1044480 | tf_op jit(solution)/shard_map/conv_general_dilated | solution.py:93
  339.7 3.2 reshape.86
  345.7 29.8 %fusion.119 = f32[16,16,3,3,3]{0,1,4,3,2:T(8,128)} fusion(bf16[16,1,6,10,130]{0,1,4,3,2:T(2,128)(2,1)} %copy.62, bf16[16,1,4,8,128]{0,1,4,3,2:T(2,128)(2,1)S(1)} %copy.63), kind=kOutput, calls=%fused_computation.274 | convolution fusion | flops 56623104 | bytes 408320 | tf_op jit(solution)/shard_map/transpose | solution.py:89
  375.5 111.1 %all-reduce.47 = (f32[16,16,3,3,3]{0,1,4,3,2:T(8,128)S(1)}, f32[16,16,3,3,3]{0,1,4,3,2:T(8,128)S(1)}, f32[16]{0:T(128)S(1)}) all-reduce(f32[16,16,3,3,3]{0,1,4,3,2:T(8,128)} %fusion.119, f32[16,16,3,3,3]{0,1,4,3,2:T(8,128)S(1)} %fusion.120, f32[16]{0:T(128)S(1)} %convolution_bitcast_fusion), channel_id=1, replica_groups=mesh['gz'=32,'gy'=16] {'gz','gy'}, use_global_device_ids=true, to_apply=%region_0.1 | all-reduce | flops 13840 | bytes 110720 | tf_op jit(solution)/shard_map/psum | solution.py:164
  495.4 6.9 %collective-permute-done.41 = bf16[16,1,10,128]{3,0,2,1:T(8,128)(2,1)S(1)} collective-permute-done((bf16[16,1,10,128]{3,0,2,1:T(8,128)(2,1)S(1)}, bf16[16,1,10,128]{3,0,2,1:T(8,128)(2,1)S(1)}, u32[]{:S(2)}, u32[]{:S(2)}) %collective-permute-start.41) | collective-permute-done | bytes 40992 | tf_op jit(solution)/shard_map/ppermute | solution.py:34
  502.5 5.4 %collective-permute-start.42 = (bf16[16,4,1,128]{3,0,2,1:T(8,128)(2,1)S(1)}, bf16[16,4,1,128]{3,0,2,1:T(8,128)(2,1)S(1)}, u32[]{:S(2)}, u32[]{:S(2)}) collective-permute-start(bf16[16,4,1,128]{3,0,2,1:T(8,128)(2,1)S(1)} %get-tuple-element.61), channel_id=1, source_target_pairs={{0,1},{1,2},{2,3},{3,4},{4,5},{5,6},{6,7},{7,8},{8,9},{9,10},{10,1... | collective-permute-start | bytes 49160 | tf_op jit(solution)/shard_map/ppermute | solution.py:34
  (210 shorter events, 99.6 us)
Async XLA Ops:
  1.5 12.1 %collective-permute-start = (bf16[16,1,8,128]{3,0,2,1:T(8,128)(2,1)S(1)}, bf16[16,1,8,128]{3,0,2,1:T(8,128)(2,1)S(1)}, u32[]{:S(2)}, u32[]{:S(2)}) collective-permute-start(bf16[16,1,8,128]{3,0,2,1:T(8,128)(2,1)S(1)} %copy.83), channel_id=1, source_target_pairs={{0,16},{16,32},{32,48},{48,64},{64,80},{80,96},{96,112},{112,128},... | collective-permute-start | bytes 98312 | tf_op jit(solution)/shard_map/ppermute | solution.py:21
  10.9 9.1 %collective-permute-start.1 = (bf16[16,1,8,128]{3,0,2,1:T(8,128)(2,1)S(1)}, bf16[16,1,8,128]{3,0,2,1:T(8,128)(2,1)S(1)}, u32[]{:S(2)}, u32[]{:S(2)}) collective-permute-start(bf16[16,1,8,128]{3,0,2,1:T(8,128)(2,1)S(1)} %copy.84), channel_id=1, source_target_pairs={{16,0},{32,16},{48,32},{64,48},{80,64},{96,80},{112,96},{128,112},... | collective-permute-start | bytes 98312 | tf_op jit(solution)/shard_map/ppermute | solution.py:22
  20.0 14.9 %collective-permute-start.2 = (bf16[16,6,1,128]{3,0,2,1:T(8,128)(2,1)S(1)}, bf16[16,6,1,128]{3,0,2,1:T(8,128)(2,1)S(1)}, u32[]{:S(2)}, u32[]{:S(2)}) collective-permute-start(bf16[16,6,1,128]{3,0,2,1:T(8,128)(2,1)S(1)} %get-tuple-element.59), channel_id=1, source_target_pairs={{0,1},{1,2},{2,3},{3,4},{4,5},{5,6},{6,7},{7,8},{8,9},{9,10},{10,1... | collective-permute-start | bytes 73736 | tf_op jit(solution)/shard_map/ppermute | solution.py:21
  23.5 11.4 %collective-permute-start.3 = (bf16[16,6,1,128]{3,0,2,1:T(8,128)(2,1)S(1)}, bf16[16,6,1,128]{3,0,2,1:T(8,128)(2,1)S(1)}, u32[]{:S(2)}, u32[]{:S(2)}) collective-permute-start(bf16[16,6,1,128]{3,0,2,1:T(8,128)(2,1)S(1)} %get-tuple-element.60), channel_id=1, source_target_pairs={{1,0},{2,1},{3,2},{4,3},{5,4},{6,5},{7,6},{8,7},{9,8},{10,9},{11,1... | collective-permute-start | bytes 73736 | tf_op jit(solution)/shard_map/ppermute | solution.py:22
  25.4 33.2 %collective-permute-start.8 = (f32[1,8,128]{2,1,0:T(8,128)S(1)}, f32[1,8,128]{2,1,0:T(8,128)S(1)}, u32[]{:S(2)}, u32[]{:S(2)}) collective-permute-start(f32[1,8,128]{2,1,0:T(8,128)S(1)} %get-tuple-element.114), channel_id=1, source_target_pairs={{16,0},{32,16},{48,32},{64,48},{80,64},{96,80},{112,96},{128,112},... | collective-permute-start | bytes 12296 | tf_op jit(solution)/shard_map/ppermute | solution.py:22
  27.4 31.3 %collective-permute-start.9 = (f32[1,8,128]{2,1,0:T(8,128)S(1)}, f32[1,8,128]{2,1,0:T(8,128)S(1)}, u32[]{:S(2)}, u32[]{:S(2)}) collective-permute-start(f32[1,8,128]{2,1,0:T(8,128)S(1)} %get-tuple-element.113), channel_id=1, source_target_pairs={{0,16},{16,32},{32,48},{48,64},{64,80},{80,96},{96,112},{112,128},... | collective-permute-start | bytes 12296 | tf_op jit(solution)/shard_map/ppermute | solution.py:21
  53.3 12.9 %collective-permute-start.4 = (bf16[16,1,8,128]{3,0,2,1:T(8,128)(2,1)S(1)}, bf16[16,1,8,128]{3,0,2,1:T(8,128)(2,1)S(1)}, u32[]{:S(2)}, u32[]{:S(2)}) collective-permute-start(bf16[16,1,8,128]{3,0,2,1:T(8,128)(2,1)S(1)} %get-tuple-element.65), channel_id=1, source_target_pairs={{0,16},{16,32},{32,48},{48,64},{64,80},{80,96},{96,112},{112,128},... | collective-permute-start | bytes 98312 | tf_op jit(solution)/shard_map/ppermute | solution.py:21
  56.7 9.4 %collective-permute-start.5 = (bf16[16,1,8,128]{3,0,2,1:T(8,128)(2,1)S(1)}, bf16[16,1,8,128]{3,0,2,1:T(8,128)(2,1)S(1)}, u32[]{:S(2)}, u32[]{:S(2)}) collective-permute-start(bf16[16,1,8,128]{3,0,2,1:T(8,128)(2,1)S(1)} %get-tuple-element.66), channel_id=1, source_target_pairs={{16,0},{32,16},{48,32},{64,48},{80,64},{96,80},{112,96},{128,112},... | collective-permute-start | bytes 98312 | tf_op jit(solution)/shard_map/ppermute | solution.py:22
  58.7 14.0 %collective-permute-start.10 = (f32[6,1,128]{2,1,0:T(1,128)S(1)}, f32[6,1,128]{2,1,0:T(1,128)S(1)}, u32[]{:S(2)}, u32[]{:S(2)}) collective-permute-start(f32[6,1,128]{2,1,0:T(1,128)S(1)} %get-tuple-element.99), channel_id=1, source_target_pairs={{1,0},{2,1},{3,2},{4,3},{5,4},{6,5},{7,6},{8,7},{9,8},{10,9},{11,1... | collective-permute-start | bytes 9224 | tf_op jit(solution)/shard_map/ppermute | solution.py:22
  61.2 11.5 %collective-permute-start.11 = (f32[6,1,128]{2,1,0:T(1,128)S(1)}, f32[6,1,128]{2,1,0:T(1,128)S(1)}, u32[]{:S(2)}, u32[]{:S(2)}) collective-permute-start(f32[6,1,128]{2,1,0:T(1,128)S(1)} %get-tuple-element.98), channel_id=1, source_target_pairs={{0,1},{1,2},{2,3},{3,4},{4,5},{5,6},{6,7},{7,8},{8,9},{9,10},{10,1... | collective-permute-start | bytes 9224 | tf_op jit(solution)/shard_map/ppermute | solution.py:21
  66.2 6.7 %collective-permute-start.6 = (bf16[16,6,1,128]{3,0,2,1:T(8,128)(2,1)S(1)}, bf16[16,6,1,128]{3,0,2,1:T(8,128)(2,1)S(1)}, u32[]{:S(2)}, u32[]{:S(2)}) collective-permute-start(bf16[16,6,1,128]{3,0,2,1:T(8,128)(2,1)S(1)} %get-tuple-element.57), channel_id=1, source_target_pairs={{0,1},{1,2},{2,3},{3,4},{4,5},{5,6},{6,7},{7,8},{8,9},{9,10},{10,1... | collective-permute-start | bytes 73736 | tf_op jit(solution)/shard_map/ppermute | solution.py:21
  70.6 6.7 %collective-permute-start.7 = (bf16[16,6,1,128]{3,0,2,1:T(8,128)(2,1)S(1)}, bf16[16,6,1,128]{3,0,2,1:T(8,128)(2,1)S(1)}, u32[]{:S(2)}, u32[]{:S(2)}) collective-permute-start(bf16[16,6,1,128]{3,0,2,1:T(8,128)(2,1)S(1)} %get-tuple-element.58), channel_id=1, source_target_pairs={{1,0},{2,1},{3,2},{4,3},{5,4},{6,5},{7,6},{8,7},{9,8},{10,9},{11,1... | collective-permute-start | bytes 73736 | tf_op jit(solution)/shard_map/ppermute | solution.py:22
  97.4 133.4 %copy-start.4 = (bf16[16,1,6,10,130]{4,0,3,2,1:T(8,128)(2,1)S(1)}, bf16[16,1,6,10,130]{4,0,3,2,1:T(8,128)(2,1)}, u32[]{:S(2)}) copy-start(bf16[16,1,6,10,130]{4,0,3,2,1:T(8,128)(2,1)} %get-tuple-element.55) | copy-start | bytes 748804
  98.0 9.8 %collective-permute-start.12 = (f32[1,8,128]{2,1,0:T(8,128)S(1)}, f32[1,8,128]{2,1,0:T(8,128)S(1)}, u32[]{:S(2)}, u32[]{:S(2)}) collective-permute-start(f32[1,8,128]{2,1,0:T(8,128)S(1)} %get-tuple-element.112), channel_id=1, source_target_pairs={{16,0},{32,16},{48,32},{64,48},{80,64},{96,80},{112,96},{128,112},... | collective-permute-start | bytes 12296 | tf_op jit(solution)/shard_map/ppermute | solution.py:22
  103.5 5.0 collective-permute-start.13
  108.5 7.4 %collective-permute-start.14 = (f32[6,1,128]{2,1,0:T(1,128)S(1)}, f32[6,1,128]{2,1,0:T(1,128)S(1)}, u32[]{:S(2)}, u32[]{:S(2)}) collective-permute-start(f32[6,1,128]{2,1,0:T(1,128)S(1)} %get-tuple-element.97), channel_id=1, source_target_pairs={{1,0},{2,1},{3,2},{4,3},{5,4},{6,5},{7,6},{8,7},{9,8},{10,9},{11,1... | collective-permute-start | bytes 9224 | tf_op jit(solution)/shard_map/ppermute | solution.py:22
  110.5 6.2 %collective-permute-start.15 = (f32[6,1,128]{2,1,0:T(1,128)S(1)}, f32[6,1,128]{2,1,0:T(1,128)S(1)}, u32[]{:S(2)}, u32[]{:S(2)}) collective-permute-start(f32[6,1,128]{2,1,0:T(1,128)S(1)} %get-tuple-element.96), channel_id=1, source_target_pairs={{0,1},{1,2},{2,3},{3,4},{4,5},{5,6},{6,7},{7,8},{8,9},{9,10},{10,1... | collective-permute-start | bytes 9224 | tf_op jit(solution)/shard_map/ppermute | solution.py:21
  116.9 120.7 %copy-start.10 = (f32[4,8,128]{2,1,0:T(8,128)}, f32[4,8,128]{2,1,0:T(8,128)S(1)}, u32[]{:S(2)}) copy-start(f32[4,8,128]{2,1,0:T(8,128)S(1)} %get-tuple-element.46) | copy-start | bytes 49156
  116.9 11.2 %collective-permute-start.16 = (f32[1,8,128]{2,1,0:T(8,128)S(1)}, f32[1,8,128]{2,1,0:T(8,128)S(1)}, u32[]{:S(2)}, u32[]{:S(2)}) collective-permute-start(f32[1,8,128]{2,1,0:T(8,128)S(1)} %get-tuple-element.110), channel_id=1, source_target_pairs={{16,0},{32,16},{48,32},{64,48},{80,64},{96,80},{112,96},{128,112},... | collective-permute-start | bytes 12296 | tf_op jit(solution)/shard_map/ppermute | solution.py:22
  125.5 3.3 collective-permute-start.17
  128.8 7.9 %collective-permute-start.18 = (f32[6,1,128]{2,1,0:T(1,128)S(1)}, f32[6,1,128]{2,1,0:T(1,128)S(1)}, u32[]{:S(2)}, u32[]{:S(2)}) collective-permute-start(f32[6,1,128]{2,1,0:T(1,128)S(1)} %get-tuple-element.95), channel_id=1, source_target_pairs={{1,0},{2,1},{3,2},{4,3},{5,4},{6,5},{7,6},{8,7},{9,8},{10,9},{11,1... | collective-permute-start | bytes 9224 | tf_op jit(solution)/shard_map/ppermute | solution.py:22
  130.7 6.7 %collective-permute-start.19 = (f32[6,1,128]{2,1,0:T(1,128)S(1)}, f32[6,1,128]{2,1,0:T(1,128)S(1)}, u32[]{:S(2)}, u32[]{:S(2)}) collective-permute-start(f32[6,1,128]{2,1,0:T(1,128)S(1)} %get-tuple-element.94), channel_id=1, source_target_pairs={{0,1},{1,2},{2,3},{3,4},{4,5},{5,6},{6,7},{7,8},{8,9},{9,10},{10,1... | collective-permute-start | bytes 9224 | tf_op jit(solution)/shard_map/ppermute | solution.py:21
  137.7 99.8 %copy-start.11 = (f32[4,8,128]{2,1,0:T(8,128)}, f32[4,8,128]{2,1,0:T(8,128)S(1)}, u32[]{:S(2)}) copy-start(f32[4,8,128]{2,1,0:T(8,128)S(1)} %get-tuple-element.44) | copy-start | bytes 49156
  137.7 11.1 %collective-permute-start.20 = (f32[1,8,128]{2,1,0:T(8,128)S(1)}, f32[1,8,128]{2,1,0:T(8,128)S(1)}, u32[]{:S(2)}, u32[]{:S(2)}) collective-permute-start(f32[1,8,128]{2,1,0:T(8,128)S(1)} %get-tuple-element.108), channel_id=1, source_target_pairs={{16,0},{32,16},{48,32},{64,48},{80,64},{96,80},{112,96},{128,112},... | collective-permute-start | bytes 12296 | tf_op jit(solution)/shard_map/ppermute | solution.py:22
  146.9 3.1 collective-permute-start.21
  150.0 7.9 %collective-permute-start.22 = (f32[6,1,128]{2,1,0:T(1,128)S(1)}, f32[6,1,128]{2,1,0:T(1,128)S(1)}, u32[]{:S(2)}, u32[]{:S(2)}) collective-permute-start(f32[6,1,128]{2,1,0:T(1,128)S(1)} %get-tuple-element.93), channel_id=1, source_target_pairs={{1,0},{2,1},{3,2},{4,3},{5,4},{6,5},{7,6},{8,7},{9,8},{10,9},{11,1... | collective-permute-start | bytes 9224 | tf_op jit(solution)/shard_map/ppermute | solution.py:22
  151.9 6.7 %collective-permute-start.23 = (f32[6,1,128]{2,1,0:T(1,128)S(1)}, f32[6,1,128]{2,1,0:T(1,128)S(1)}, u32[]{:S(2)}, u32[]{:S(2)}) collective-permute-start(f32[6,1,128]{2,1,0:T(1,128)S(1)} %get-tuple-element.92), channel_id=1, source_target_pairs={{0,1},{1,2},{2,3},{3,4},{4,5},{5,6},{6,7},{7,8},{8,9},{9,10},{10,1... | collective-permute-start | bytes 9224 | tf_op jit(solution)/shard_map/ppermute | solution.py:21
  159.8 11.4 %collective-permute-start.24 = (bf16[1,10,128]{2,1,0:T(8,128)(2,1)S(1)}, bf16[1,10,128]{2,1,0:T(8,128)(2,1)S(1)}, u32[]{:S(2)}, u32[]{:S(2)}) collective-permute-start(bf16[1,10,128]{2,1,0:T(8,128)(2,1)S(1)} %get-tuple-element.85), channel_id=1, source_target_pairs={{0,16},{16,32},{32,48},{48,64},{64,80},{80,96},{96,112},{112,128},... | collective-permute-start | bytes 7688 | tf_op jit(solution)/shard_map/ppermute | solution.py:34
  168.4 8.8 %collective-permute-start.25 = (bf16[1,10,128]{2,1,0:T(8,128)(2,1)S(1)}, bf16[1,10,128]{2,1,0:T(8,128)(2,1)S(1)}, u32[]{:S(2)}, u32[]{:S(2)}) collective-permute-start(bf16[1,10,128]{2,1,0:T(8,128)(2,1)S(1)} %get-tuple-element.86), channel_id=1, source_target_pairs={{16,0},{32,16},{48,32},{64,48},{80,64},{96,80},{112,96},{128,112},... | collective-permute-start | bytes 7688 | tf_op jit(solution)/shard_map/ppermute | solution.py:34
  177.3 8.0 %collective-permute-start.26 = (bf16[4,1,128]{2,1,0:T(2,128)(2,1)S(1)}, bf16[4,1,128]{2,1,0:T(2,128)(2,1)S(1)}, u32[]{:S(2)}, u32[]{:S(2)}) collective-permute-start(bf16[4,1,128]{2,1,0:T(2,128)(2,1)S(1)} %get-tuple-element.104), channel_id=1, source_target_pairs={{0,1},{1,2},{2,3},{3,4},{4,5},{5,6},{6,7},{7,8},{8,9},{9,10},{10,1... | collective-permute-start | bytes 3080 | tf_op jit(solution)/shard_map/ppermute | solution.py:34
  183.3 6.4 %collective-permute-start.27 = (bf16[4,1,128]{2,1,0:T(2,128)(2,1)S(1)}, bf16[4,1,128]{2,1,0:T(2,128)(2,1)S(1)}, u32[]{:S(2)}, u32[]{:S(2)}) collective-permute-start(bf16[4,1,128]{2,1,0:T(2,128)(2,1)S(1)} %get-tuple-element.105), channel_id=1, source_target_pairs={{1,0},{2,1},{3,2},{4,3},{5,4},{6,5},{7,6},{8,7},{9,8},{10,9},{11,1... | collective-permute-start | bytes 3080 | tf_op jit(solution)/shard_map/ppermute | solution.py:34
  190.5 7.1 %collective-permute-start.28 = (bf16[1,10,128]{2,1,0:T(8,128)(2,1)S(1)}, bf16[1,10,128]{2,1,0:T(8,128)(2,1)S(1)}, u32[]{:S(2)}, u32[]{:S(2)}) collective-permute-start(bf16[1,10,128]{2,1,0:T(8,128)(2,1)S(1)} %get-tuple-element.83), channel_id=1, source_target_pairs={{0,16},{16,32},{32,48},{48,64},{64,80},{80,96},{96,112},{112,128},... | collective-permute-start | bytes 7688 | tf_op jit(solution)/shard_map/ppermute | solution.py:34
  193.9 9.1 %collective-permute-start.29 = (bf16[1,10,128]{2,1,0:T(8,128)(2,1)S(1)}, bf16[1,10,128]{2,1,0:T(8,128)(2,1)S(1)}, u32[]{:S(2)}, u32[]{:S(2)}) collective-permute-start(bf16[1,10,128]{2,1,0:T(8,128)(2,1)S(1)} %get-tuple-element.84), channel_id=1, source_target_pairs={{16,0},{32,16},{48,32},{64,48},{80,64},{96,80},{112,96},{128,112},... | collective-permute-start | bytes 7688 | tf_op jit(solution)/shard_map/ppermute | solution.py:34
  203.1 5.3 %collective-permute-start.30 = (bf16[4,1,128]{2,1,0:T(2,128)(2,1)S(1)}, bf16[4,1,128]{2,1,0:T(2,128)(2,1)S(1)}, u32[]{:S(2)}, u32[]{:S(2)}) collective-permute-start(bf16[4,1,128]{2,1,0:T(2,128)(2,1)S(1)} %get-tuple-element.102), channel_id=1, source_target_pairs={{0,1},{1,2},{2,3},{3,4},{4,5},{5,6},{6,7},{7,8},{8,9},{9,10},{10,1... | collective-permute-start | bytes 3080 | tf_op jit(solution)/shard_map/ppermute | solution.py:34
  205.1 6.4 %collective-permute-start.31 = (bf16[4,1,128]{2,1,0:T(2,128)(2,1)S(1)}, bf16[4,1,128]{2,1,0:T(2,128)(2,1)S(1)}, u32[]{:S(2)}, u32[]{:S(2)}) collective-permute-start(bf16[4,1,128]{2,1,0:T(2,128)(2,1)S(1)} %get-tuple-element.103), channel_id=1, source_target_pairs={{1,0},{2,1},{3,2},{4,3},{5,4},{6,5},{7,6},{8,7},{9,8},{10,9},{11,1... | collective-permute-start | bytes 3080 | tf_op jit(solution)/shard_map/ppermute | solution.py:34
  212.3 7.4 %collective-permute-start.32 = (bf16[1,10,128]{2,1,0:T(8,128)(2,1)S(1)}, bf16[1,10,128]{2,1,0:T(8,128)(2,1)S(1)}, u32[]{:S(2)}, u32[]{:S(2)}) collective-permute-start(bf16[1,10,128]{2,1,0:T(8,128)(2,1)S(1)} %get-tuple-element.81), channel_id=1, source_target_pairs={{0,16},{16,32},{32,48},{48,64},{64,80},{80,96},{96,112},{112,128},... | collective-permute-start | bytes 7688 | tf_op jit(solution)/shard_map/ppermute | solution.py:34
  215.1 8.8 %collective-permute-start.33 = (bf16[1,10,128]{2,1,0:T(8,128)(2,1)S(1)}, bf16[1,10,128]{2,1,0:T(8,128)(2,1)S(1)}, u32[]{:S(2)}, u32[]{:S(2)}) collective-permute-start(bf16[1,10,128]{2,1,0:T(8,128)(2,1)S(1)} %get-tuple-element.82), channel_id=1, source_target_pairs={{16,0},{32,16},{48,32},{64,48},{80,64},{96,80},{112,96},{128,112},... | collective-permute-start | bytes 7688 | tf_op jit(solution)/shard_map/ppermute | solution.py:34
  225.3 22.1 %collective-permute-start.34 = (bf16[4,1,128]{2,1,0:T(2,128)(2,1)}, bf16[4,1,128]{2,1,0:T(2,128)(2,1)}, u32[]{:S(2)}, u32[]{:S(2)}) collective-permute-start(bf16[4,1,128]{2,1,0:T(2,128)(2,1)} %get-tuple-element.100), channel_id=1, source_target_pairs={{0,1},{1,2},{2,3},{3,4},{4,5},{5,6},{6,7},{7,8},{8,9},{9,10},{10,1... | collective-permute-start | bytes 3080 | tf_op jit(solution)/shard_map/ppermute | solution.py:34
  227.2 20.1 %collective-permute-start.35 = (bf16[4,1,128]{2,1,0:T(2,128)(2,1)}, bf16[4,1,128]{2,1,0:T(2,128)(2,1)}, u32[]{:S(2)}, u32[]{:S(2)}) collective-permute-start(bf16[4,1,128]{2,1,0:T(2,128)(2,1)} %get-tuple-element.101), channel_id=1, source_target_pairs={{1,0},{2,1},{3,2},{4,3},{5,4},{6,5},{7,6},{8,7},{9,8},{10,9},{11,1... | collective-permute-start | bytes 3080 | tf_op jit(solution)/shard_map/ppermute | solution.py:34
  275.1 38.1 %collective-permute-start.36 = (bf16[16,1,10,128]{3,0,2,1:T(8,128)(2,1)S(1)}, bf16[16,1,10,128]{3,0,2,1:T(8,128)(2,1)S(1)}, u32[]{:S(2)}, u32[]{:S(2)}) collective-permute-start(bf16[16,1,10,128]{3,0,2,1:T(8,128)(2,1)S(1)} %get-tuple-element.51), channel_id=1, source_target_pairs={{0,16},{16,32},{32,48},{48,64},{64,80},{80,96},{96,112},{112,128},... | collective-permute-start | bytes 122888 | tf_op jit(solution)/shard_map/ppermute | solution.py:34
  277.6 35.6 %collective-permute-start.37 = (bf16[16,1,10,128]{3,0,2,1:T(8,128)(2,1)S(1)}, bf16[16,1,10,128]{3,0,2,1:T(8,128)(2,1)S(1)}, u32[]{:S(2)}, u32[]{:S(2)}) collective-permute-start(bf16[16,1,10,128]{3,0,2,1:T(8,128)(2,1)S(1)} %get-tuple-element.52), channel_id=1, source_target_pairs={{16,0},{32,16},{48,32},{64,48},{80,64},{96,80},{112,96},{128,112},... | collective-permute-start | bytes 122888 | tf_op jit(solution)/shard_map/ppermute | solution.py:34
  313.4 6.1 %collective-permute-start.38 = (bf16[16,4,1,128]{3,0,2,1:T(8,128)(2,1)S(1)}, bf16[16,4,1,128]{3,0,2,1:T(8,128)(2,1)S(1)}, u32[]{:S(2)}, u32[]{:S(2)}) collective-permute-start(bf16[16,4,1,128]{3,0,2,1:T(8,128)(2,1)S(1)} %get-tuple-element.63), channel_id=1, source_target_pairs={{0,1},{1,2},{2,3},{3,4},{4,5},{5,6},{6,7},{7,8},{8,9},{9,10},{10,1... | collective-permute-start | bytes 49160 | tf_op jit(solution)/shard_map/ppermute | solution.py:34
  317.1 6.6 %collective-permute-start.39 = (bf16[16,4,1,128]{3,0,2,1:T(8,128)(2,1)S(1)}, bf16[16,4,1,128]{3,0,2,1:T(8,128)(2,1)S(1)}, u32[]{:S(2)}, u32[]{:S(2)}) collective-permute-start(bf16[16,4,1,128]{3,0,2,1:T(8,128)(2,1)S(1)} %get-tuple-element.64), channel_id=1, source_target_pairs={{1,0},{2,1},{3,2},{4,3},{5,4},{6,5},{7,6},{8,7},{9,8},{10,9},{11,1... | collective-permute-start | bytes 49160 | tf_op jit(solution)/shard_map/ppermute | solution.py:34
  375.5 140.0 %copy-start.1 = (bf16[16,16,3,3,3]{1,0,4,3,2:T(8,128)(2,1)S(1)}, bf16[16,16,3,3,3]{1,0,4,3,2:T(8,128)(2,1)}, u32[]{:S(2)}) copy-start(bf16[16,16,3,3,3]{1,0,4,3,2:T(8,128)(2,1)} %param.10) | copy-start | bytes 41476
  491.0 4.4 collective-permute-start.40
  492.9 9.4 %collective-permute-start.41 = (bf16[16,1,10,128]{3,0,2,1:T(8,128)(2,1)S(1)}, bf16[16,1,10,128]{3,0,2,1:T(8,128)(2,1)S(1)}, u32[]{:S(2)}, u32[]{:S(2)}) collective-permute-start(bf16[16,1,10,128]{3,0,2,1:T(8,128)(2,1)S(1)} %get-tuple-element.50), channel_id=1, source_target_pairs={{16,0},{32,16},{48,32},{64,48},{80,64},{96,80},{112,96},{128,112},... | collective-permute-start | bytes 122888 | tf_op jit(solution)/shard_map/ppermute | solution.py:34
  502.5 9.5 %collective-permute-start.42 = (bf16[16,4,1,128]{3,0,2,1:T(8,128)(2,1)S(1)}, bf16[16,4,1,128]{3,0,2,1:T(8,128)(2,1)S(1)}, u32[]{:S(2)}, u32[]{:S(2)}) collective-permute-start(bf16[16,4,1,128]{3,0,2,1:T(8,128)(2,1)S(1)} %get-tuple-element.61), channel_id=1, source_target_pairs={{0,1},{1,2},{2,3},{3,4},{4,5},{5,6},{6,7},{7,8},{8,9},{9,10},{10,1... | collective-permute-start | bytes 49160 | tf_op jit(solution)/shard_map/ppermute | solution.py:34
  507.9 6.9 %collective-permute-start.43 = (bf16[16,4,1,128]{3,0,2,1:T(8,128)(2,1)S(1)}, bf16[16,4,1,128]{3,0,2,1:T(8,128)(2,1)S(1)}, u32[]{:S(2)}, u32[]{:S(2)}) collective-permute-start(bf16[16,4,1,128]{3,0,2,1:T(8,128)(2,1)S(1)} %get-tuple-element.62), channel_id=1, source_target_pairs={{1,0},{2,1},{3,2},{4,3},{5,4},{6,5},{7,6},{8,7},{9,8},{10,9},{11,1... | collective-permute-start | bytes 49160 | tf_op jit(solution)/shard_map/ppermute | solution.py:34
  (22 other events, 448.4 us)
where the time goes:
time: 524 us; the launch traced here: 516 us
  starting transfers between devices  171 us (33%)
  blocking collectives  111 us (21%)
  matrix products  86.3 us (16%)
  local copies, waits for them, and re-layouts  78.4 us (15%)
  waiting for transfers between devices  51.9 us (10%)
  other arithmetic  12.8 us (2%)
    psum x1, blocking collectives, on_device(): lax.psum((raw_first, raw_second, raw_speed), ('gz', 'gy'))  111 us
    ppermute x20, starting transfers between devices, from_behind(): return lax.ppermute(block, axis, route)  70.3 us
    ppermute x12, starting transfers between devices, extended(): before = lax.ppermute(last, axis, up)  59.5 us
    transpose x2, matrix products, weight_grad(): return d_weight.transpose(1, 0, 2, 3, 4)  59.3 us
    ppermute x12, starting transfers between devices, extended(): after = lax.ppermute(initial, axis, down)  41.2 us
    ppermute x20, waiting for transfers between devices, from_behind(): return lax.ppermute(block, axis, route)  37.2 us
    conv_general_dilated x10, local copies, waits for them, and re-layouts, conv_back(): lax.conv_general_dilated(d_out[None], flip_weight(weight), (1, 1, 1), ((2...  25.9 us
    conv_general_dilated x12, local copies, waits for them, and re-layouts, conv_local(): lax.conv_general_dilated(grid[None], weight, (1, 1, 1), 'VALID', dimensio...  22 us
  transfers between devices with their start and end apart: 44, of which 16 were waited for; matrix products, arithmetic and copies ran while one was open for 13% of the time, Pallas kernels for 0%

commit v1 on v0

--- a/solution.py
+++ b/solution.py
@@ -161,7 +161,9 @@
     d_first = (d_hidden * silu_slope(act_first)).astype(jnp.bfloat16)
     raw_first = weight_grad(feat_pad, d_first)
     d_feat = input_grad(conv_first, d_first)
-    raw_first, raw_second, raw_speed = lax.psum((raw_first, raw_second, raw_speed), ("gz", "gy"))
+    raw_first, raw_second, raw_speed = lax.psum(
+        lax.psum((raw_first, raw_second, raw_speed), "gz"), "gy"
+    )
     total = (
         jnp.sum(raw_first * raw_first)
         + jnp.sum(raw_second * raw_second)

time: 524 us -> 654 us (1.25)
  the two profiles are of different devices: /device:TPU:15 before, /device:TPU:1 now
where the time goes in v1:
time: 654 us; the launch traced here: 646 us
  blocking collectives  235 us (36%)
  starting transfers between devices  174 us (27%)
  matrix products  86.5 us (13%)
  local copies, waits for them, and re-layouts  78.3 us (12%)
  waiting for transfers between devices  54.9 us (8%)
  other arithmetic  12.8 us (2%)
    psum x1, blocking collectives, on_device(): lax.psum((raw_first, raw_second, raw_speed), 'gz')  169 us
    ppermute x20, starting transfers between devices, from_behind(): return lax.ppermute(block, axis, route)  81.5 us
    ppermute x12, starting transfers between devices, extended(): before = lax.ppermute(last, axis, up)  73.4 us
    psum x1, blocking collectives, on_device(): lax.psum(lax.psum((raw_first, raw_second, raw_speed), 'gz'), 'gy')  66 us
    transpose x2, matrix products, weight_grad(): return d_weight.transpose(1, 0, 2, 3, 4)  59.5 us
    ppermute x20, waiting for transfers between devices, from_behind(): return lax.ppermute(block, axis, route)  40.9 us
    conv_general_dilated x10, local copies, waits for them, and re-layouts, conv_back(): lax.conv_general_dilated(d_out[None], flip_weight(weight), (1, 1, 1), ((2...  25.9 us
    conv_general_dilated x12, local copies, waits for them, and re-layouts, conv_local(): lax.conv_general_dilated(grid[None], weight, (1, 1, 1), 'VALID', dimensio...  22 us
  transfers between devices with their start and end apart: 44, of which 17 were waited for; matrix products, arithmetic and copies ran while one was open for 11% of the time, Pallas kernels for 0%

profile of v1, /device:TPU:1, one launch (start us, length us, event | category | flops | bytes accessed | tf_op | source)
XLA Modules:
  0.0 646.0 jit_solution(11685186355057886530)
XLA Ops:
  1.5 10.2 %collective-permute-start = (bf16[16,1,8,128]{3,0,2,1:T(8,128)(2,1)S(1)}, bf16[16,1,8,128]{3,0,2,1:T(8,128)(2,1)S(1)}, u32[]{:S(2)}, u32[]{:S(2)}) collective-permute-start(bf16[16,1,8,128]{3,0,2,1:T(8,128)(2,1)S(1)} %copy.83), channel_id=1, source_target_pairs={{0,16},{16,32},{32,48},{48,64},{64,80},{80,96},{96,112},{112,128},... | collective-permute-start | bytes 98312 | tf_op jit(solution)/shard_map/ppermute | solution.py:21
  15.3 5.5 collective-permute-done.1
  20.9 3.1 collective-permute-start.2
  27.2 7.5 %collective-permute-start.9 = (f32[1,8,128]{2,1,0:T(8,128)S(1)}, f32[1,8,128]{2,1,0:T(8,128)S(1)}, u32[]{:S(2)}, u32[]{:S(2)}) collective-permute-start(f32[1,8,128]{2,1,0:T(8,128)S(1)} %get-tuple-element.116), channel_id=1, source_target_pairs={{0,16},{16,32},{32,48},{48,64},{64,80},{80,96},{96,112},{112,128},... | collective-permute-start | bytes 12296 | tf_op jit(solution)/shard_map/ppermute | solution.py:21
  37.4 4.2 copy.46
  42.7 5.8 fusion.6
  48.5 2.9 copy.47
  53.1 3.6 collective-permute-start.4
  59.9 4.6 collective-permute-start.11
  65.8 4.0 collective-permute-start.6
  71.5 2.9 collective-permute-done.7
  77.0 4.2 copy.50
  82.3 5.8 fusion.10
  97.0 7.9 %collective-permute-start.13 = (f32[1,8,128]{2,1,0:T(8,128)S(1)}, f32[1,8,128]{2,1,0:T(8,128)S(1)}, u32[]{:S(2)}, u32[]{:S(2)}) collective-permute-start(f32[1,8,128]{2,1,0:T(8,128)S(1)} %get-tuple-element.114), channel_id=1, source_target_pairs={{0,16},{16,32},{32,48},{48,64},{64,80},{80,96},{96,112},{112,128},... | collective-permute-start | bytes 12296 | tf_op jit(solution)/shard_map/ppermute | solution.py:21
  106.9 4.8 collective-permute-start.15
  114.7 8.9 %collective-permute-start.17 = (f32[1,8,128]{2,1,0:T(8,128)S(1)}, f32[1,8,128]{2,1,0:T(8,128)S(1)}, u32[]{:S(2)}, u32[]{:S(2)}) collective-permute-start(f32[1,8,128]{2,1,0:T(8,128)S(1)} %get-tuple-element.112), channel_id=1, source_target_pairs={{0,16},{16,32},{32,48},{48,64},{64,80},{80,96},{96,112},{112,128},... | collective-permute-start | bytes 12296 | tf_op jit(solution)/shard_map/ppermute | solution.py:21
  125.7 4.5 collective-permute-start.19
  133.1 8.9 %collective-permute-start.21 = (f32[1,8,128]{2,1,0:T(8,128)S(1)}, f32[1,8,128]{2,1,0:T(8,128)S(1)}, u32[]{:S(2)}, u32[]{:S(2)}) collective-permute-start(f32[1,8,128]{2,1,0:T(8,128)S(1)} %get-tuple-element.110), channel_id=1, source_target_pairs={{0,16},{16,32},{32,48},{48,64},{64,80},{80,96},{96,112},{112,128},... | collective-permute-start | bytes 12296 | tf_op jit(solution)/shard_map/ppermute | solution.py:21
  144.1 5.2 collective-permute-start.23
  151.2 8.9 %collective-permute-start.24 = (bf16[1,10,128]{2,1,0:T(8,128)(2,1)S(1)}, bf16[1,10,128]{2,1,0:T(8,128)(2,1)S(1)}, u32[]{:S(2)}, u32[]{:S(2)}) collective-permute-start(bf16[1,10,128]{2,1,0:T(8,128)(2,1)S(1)} %get-tuple-element.88), channel_id=1, source_target_pairs={{0,16},{16,32},{32,48},{48,64},{64,80},{80,96},{96,112},{112,128},... | collective-permute-start | bytes 7688 | tf_op jit(solution)/shard_map/ppermute | solution.py:34
  162.1 6.9 %collective-permute-done.25 = bf16[1,10,128]{2,1,0:T(8,128)(2,1)S(1)} collective-permute-done((bf16[1,10,128]{2,1,0:T(8,128)(2,1)S(1)}, bf16[1,10,128]{2,1,0:T(8,128)(2,1)S(1)}, u32[]{:S(2)}, u32[]{:S(2)}) %collective-permute-start.25) | collective-permute-done | bytes 2592 | tf_op jit(solution)/shard_map/ppermute | solution.py:34
  169.1 5.7 collective-permute-start.26
  176.2 5.7 collective-permute-done.27
  182.7 3.1 collective-permute-start.28
  187.7 6.9 %collective-permute-done.29 = bf16[1,10,128]{2,1,0:T(8,128)(2,1)S(1)} collective-permute-done((bf16[1,10,128]{2,1,0:T(8,128)(2,1)S(1)}, bf16[1,10,128]{2,1,0:T(8,128)(2,1)S(1)}, u32[]{:S(2)}, u32[]{:S(2)}) %collective-permute-start.29) | collective-permute-done | bytes 2592 | tf_op jit(solution)/shard_map/ppermute | solution.py:34
  194.7 6.0 collective-permute-start.30
  202.1 5.7 collective-permute-done.31
  208.5 3.1 collective-permute-start.32
  213.6 6.9 %collective-permute-done.33 = bf16[1,10,128]{2,1,0:T(8,128)(2,1)S(1)} collective-permute-done((bf16[1,10,128]{2,1,0:T(8,128)(2,1)S(1)}, bf16[1,10,128]{2,1,0:T(8,128)(2,1)S(1)}, u32[]{:S(2)}, u32[]{:S(2)}) %collective-permute-start.33) | collective-permute-done | bytes 2592 | tf_op jit(solution)/shard_map/ppermute | solution.py:34
  221.7 6.3 collective-permute-start.34
  229.6 6.7 %copy.62 = bf16[16,1,6,10,130]{0,1,4,3,2:T(2,128)(2,1)} copy(bf16[16,1,6,10,130]{4,0,3,2,1:T(8,128)(2,1)S(1)} %copy-done.4) | data formatting | bytes 499200 | tf_op jit(solution)/shard_map/broadcast_in_dim | solution.py:82
  236.3 6.7 %copy.64 = bf16[16,1,6,10,130]{0,1,4,3,2:T(2,128)(2,1)} copy(bf16[16,1,6,10,130]{4,0,3,2,1:T(8,128)(2,1)S(1)} %copy-done.5) | data formatting | bytes 499200 | tf_op jit(solution)/shard_map/broadcast_in_dim | solution.py:82
  247.9 3.8 copy.65
  256.3 8.0 %convolution_select_fusion.1 = f32[6,10,8,17,16]{4,2,3,1,0:T(8,128)} fusion(bf16[16,16,3,3,3]{1,0,4,3,2:T(8,128)(2,1)S(1)} %copy-done, pred[8,17]{0,1:T(8,128)(4,1)S(1)} %copy-done.25, bf16[16,4,8,1,7,2]{0,4,5,2,1,3:T(8,128)(2,1)S(1)} %slice.482, bf16[16,4,8,1,8,17]{0,4,5,2,1,3:T(8,128)(2,1)} %copy.56), kind=kOutput, calls=%fused_computation.19 | convolution fusion | flops 60759552 | bytes 689800 | tf_op jit(solution)/shard_map/conv_general_dilated | solution.py:93
  264.2 6.2 copy.57
  270.5 3.2 reshape.79
  278.6 29.5 %fusion.120 = f32[16,16,3,3,3]{0,1,4,3,2:T(8,128)S(1)} fusion(bf16[16,1,6,10,130]{0,1,4,3,2:T(2,128)(2,1)} %copy.64, bf16[16,1,4,8,128]{0,1,4,3,2:T(2,128)(2,1)} %copy.65), kind=kOutput, calls=%fused_computation.275 | convolution fusion | flops 56623104 | bytes 408320 | tf_op jit(solution)/shard_map/transpose | solution.py:89
  308.4 4.1 collective-permute-start.38
  314.2 3.2 collective-permute-done.39
  320.4 6.8 %convolution_select_fusion = f32[6,10,8,17,16]{4,2,3,1,0:T(8,128)} fusion(bf16[16,16,3,3,3]{1,0,4,3,2:T(8,128)(2,1)S(1)} %copy-done.24, pred[8,17]{0,1:T(8,128)(4,1)S(1)} %copy-done.25, bf16[16,4,8,1,7,2]{0,4,5,2,1,3:T(8,128)(2,1)S(1)} %slice.490, bf16[16,4,8,1,8,17]{0,4,5,2,1,3:T(8,128)(2,1)S(1)} %copy.60), kind=kOutput, calls=%fused_computation.18 | convolution fusion | flops 60759552 | bytes 689800 | tf_op jit(solution)/shard_map/conv_general_dilated | solution.py:93
  327.1 6.3 copy.61
  333.4 3.2 reshape.86
  339.5 29.9 %fusion.119 = f32[16,16,3,3,3]{0,1,4,3,2:T(8,128)} fusion(bf16[16,1,6,10,130]{0,1,4,3,2:T(2,128)(2,1)} %copy.62, bf16[16,1,4,8,128]{0,1,4,3,2:T(2,128)(2,1)S(1)} %copy.63), kind=kOutput, calls=%fused_computation.274 | convolution fusion | flops 56623104 | bytes 408320 | tf_op jit(solution)/shard_map/transpose | solution.py:89
  369.4 169.0 %all-reduce.47 = (f32[16,16,3,3,3]{0,1,4,3,2:T(8,128)S(1)}, f32[16,16,3,3,3]{0,1,4,3,2:T(8,128)S(1)}, f32[16]{0:T(128)S(1)}) all-reduce(f32[16,16,3,3,3]{0,1,4,3,2:T(8,128)} %fusion.119, f32[16,16,3,3,3]{0,1,4,3,2:T(8,128)S(1)} %fusion.120, f32[16]{0:T(128)S(1)} %convolution_bitcast_fusion), channel_id=1, replica_groups=mesh['gz'=32,'gy'=16] {'gz'}, use_global_device_ids=true, to_apply=%region_0.1 | all-reduce | flops 13840 | bytes 110720 | tf_op jit(solution)/shard_map/psum | solution.py:165
  538.4 66.0 %all-reduce.48 = (f32[16,16,3,3,3]{0,1,4,3,2:T(8,128)S(1)}, f32[16,16,3,3,3]{0,1,4,3,2:T(8,128)S(1)}, f32[16]{0:T(128)S(1)}) all-reduce(f32[16,16,3,3,3]{0,1,4,3,2:T(8,128)S(1)} %get-tuple-element.16, f32[16,16,3,3,3]{0,1,4,3,2:T(8,128)S(1)} %get-tuple-element.17, f32[16]{0:T(128)S(1)} %get-tuple-element.18), channel_id=1, replica_groups=mesh['gz'=32,'gy'=16] {'gy'}, use_global_device_ids=true, to_apply=%region_1.2 | all-reduce | flops 13840 | bytes 110720 | tf_op jit(solution)/shard_map/psum | solution.py:164
  608.7 21.2 %collective-permute-start.40 = (bf16[16,1,10,128]{3,0,2,1:T(8,128)(2,1)S(1)}, bf16[16,1,10,128]{3,0,2,1:T(8,128)(2,1)S(1)}, u32[]{:S(2)}, u32[]{:S(2)}) collective-permute-start(bf16[16,1,10,128]{3,0,2,1:T(8,128)(2,1)S(1)} %get-tuple-element.52), channel_id=1, source_target_pairs={{0,16},{16,32},{32,48},{48,64},{64,80},{80,96},{96,112},{112,128},... | collective-permute-start | bytes 122888 | tf_op jit(solution)/shard_map/ppermute | solution.py:34
  629.9 4.6 collective-permute-start.41
  634.5 4.6 collective-permute-done.41
  (211 shorter events, 89.0 us)
Async XLA Ops:
  1.5 12.9 %collective-permute-start = (bf16[16,1,8,128]{3,0,2,1:T(8,128)(2,1)S(1)}, bf16[16,1,8,128]{3,0,2,1:T(8,128)(2,1)S(1)}, u32[]{:S(2)}, u32[]{:S(2)}) collective-permute-start(bf16[16,1,8,128]{3,0,2,1:T(8,128)(2,1)S(1)} %copy.83), channel_id=1, source_target_pairs={{0,16},{16,32},{32,48},{48,64},{64,80},{80,96},{96,112},{112,128},... | collective-permute-start | bytes 98312 | tf_op jit(solution)/shard_map/ppermute | solution.py:21
  11.7 9.1 %collective-permute-start.1 = (bf16[16,1,8,128]{3,0,2,1:T(8,128)(2,1)S(1)}, bf16[16,1,8,128]{3,0,2,1:T(8,128)(2,1)S(1)}, u32[]{:S(2)}, u32[]{:S(2)}) collective-permute-start(bf16[16,1,8,128]{3,0,2,1:T(8,128)(2,1)S(1)} %copy.84), channel_id=1, source_target_pairs={{16,0},{32,16},{48,32},{64,48},{80,64},{96,80},{112,96},{128,112},... | collective-permute-start | bytes 98312 | tf_op jit(solution)/shard_map/ppermute | solution.py:22
  20.9 13.9 %collective-permute-start.2 = (bf16[16,6,1,128]{3,0,2,1:T(8,128)(2,1)S(1)}, bf16[16,6,1,128]{3,0,2,1:T(8,128)(2,1)S(1)}, u32[]{:S(2)}, u32[]{:S(2)}) collective-permute-start(bf16[16,6,1,128]{3,0,2,1:T(8,128)(2,1)S(1)} %get-tuple-element.62), channel_id=1, source_target_pairs={{0,1},{1,2},{2,3},{3,4},{4,5},{5,6},{6,7},{7,8},{8,9},{9,10},{10,1... | collective-permute-start | bytes 73736 | tf_op jit(solution)/shard_map/ppermute | solution.py:21
  24.0 10.8 %collective-permute-start.3 = (bf16[16,6,1,128]{3,0,2,1:T(8,128)(2,1)S(1)}, bf16[16,6,1,128]{3,0,2,1:T(8,128)(2,1)S(1)}, u32[]{:S(2)}, u32[]{:S(2)}) collective-permute-start(bf16[16,6,1,128]{3,0,2,1:T(8,128)(2,1)S(1)} %get-tuple-element.63), channel_id=1, source_target_pairs={{1,0},{2,1},{3,2},{4,3},{5,4},{6,5},{7,6},{8,7},{9,8},{10,9},{11,1... | collective-permute-start | bytes 73736 | tf_op jit(solution)/shard_map/ppermute | solution.py:22
  25.3 33.3 %collective-permute-start.8 = (f32[1,8,128]{2,1,0:T(8,128)S(1)}, f32[1,8,128]{2,1,0:T(8,128)S(1)}, u32[]{:S(2)}, u32[]{:S(2)}) collective-permute-start(f32[1,8,128]{2,1,0:T(8,128)S(1)} %get-tuple-element.117), channel_id=1, source_target_pairs={{16,0},{32,16},{48,32},{64,48},{80,64},{96,80},{112,96},{128,112},... | collective-permute-start | bytes 12296 | tf_op jit(solution)/shard_map/ppermute | solution.py:22
  27.2 31.4 %collective-permute-start.9 = (f32[1,8,128]{2,1,0:T(8,128)S(1)}, f32[1,8,128]{2,1,0:T(8,128)S(1)}, u32[]{:S(2)}, u32[]{:S(2)}) collective-permute-start(f32[1,8,128]{2,1,0:T(8,128)S(1)} %get-tuple-element.116), channel_id=1, source_target_pairs={{0,16},{16,32},{32,48},{48,64},{64,80},{80,96},{96,112},{112,128},... | collective-permute-start | bytes 12296 | tf_op jit(solution)/shard_map/ppermute | solution.py:21
  53.1 11.5 %collective-permute-start.4 = (bf16[16,1,8,128]{3,0,2,1:T(8,128)(2,1)S(1)}, bf16[16,1,8,128]{3,0,2,1:T(8,128)(2,1)S(1)}, u32[]{:S(2)}, u32[]{:S(2)}) collective-permute-start(bf16[16,1,8,128]{3,0,2,1:T(8,128)(2,1)S(1)} %get-tuple-element.68), channel_id=1, source_target_pairs={{0,16},{16,32},{32,48},{48,64},{64,80},{80,96},{96,112},{112,128},... | collective-permute-start | bytes 98312 | tf_op jit(solution)/shard_map/ppermute | solution.py:21
  56.7 9.1 %collective-permute-start.5 = (bf16[16,1,8,128]{3,0,2,1:T(8,128)(2,1)S(1)}, bf16[16,1,8,128]{3,0,2,1:T(8,128)(2,1)S(1)}, u32[]{:S(2)}, u32[]{:S(2)}) collective-permute-start(bf16[16,1,8,128]{3,0,2,1:T(8,128)(2,1)S(1)} %get-tuple-element.69), channel_id=1, source_target_pairs={{16,0},{32,16},{48,32},{64,48},{80,64},{96,80},{112,96},{128,112},... | collective-permute-start | bytes 98312 | tf_op jit(solution)/shard_map/ppermute | solution.py:22
  58.6 12.6 %collective-permute-start.10 = (f32[6,1,128]{2,1,0:T(1,128)S(1)}, f32[6,1,128]{2,1,0:T(1,128)S(1)}, u32[]{:S(2)}, u32[]{:S(2)}) collective-permute-start(f32[6,1,128]{2,1,0:T(1,128)S(1)} %get-tuple-element.102), channel_id=1, source_target_pairs={{1,0},{2,1},{3,2},{4,3},{5,4},{6,5},{7,6},{8,7},{9,8},{10,9},{11,1... | collective-permute-start | bytes 9224 | tf_op jit(solution)/shard_map/ppermute | solution.py:22
  59.9 11.4 %collective-permute-start.11 = (f32[6,1,128]{2,1,0:T(1,128)S(1)}, f32[6,1,128]{2,1,0:T(1,128)S(1)}, u32[]{:S(2)}, u32[]{:S(2)}) collective-permute-start(f32[6,1,128]{2,1,0:T(1,128)S(1)} %get-tuple-element.101), channel_id=1, source_target_pairs={{0,1},{1,2},{2,3},{3,4},{4,5},{5,6},{6,7},{7,8},{8,9},{9,10},{10,1... | collective-permute-start | bytes 9224 | tf_op jit(solution)/shard_map/ppermute | solution.py:21
  65.8 5.7 collective-permute-start.6
  69.8 4.6 collective-permute-start.7
  94.5 135.0 %copy-start.4 = (bf16[16,1,6,10,130]{4,0,3,2,1:T(8,128)(2,1)S(1)}, bf16[16,1,6,10,130]{4,0,3,2,1:T(8,128)(2,1)}, u32[]{:S(2)}) copy-start(bf16[16,1,6,10,130]{4,0,3,2,1:T(8,128)(2,1)} %get-tuple-element.58) | copy-start | bytes 748804
  95.1 9.8 %collective-permute-start.12 = (f32[1,8,128]{2,1,0:T(8,128)S(1)}, f32[1,8,128]{2,1,0:T(8,128)S(1)}, u32[]{:S(2)}, u32[]{:S(2)}) collective-permute-start(f32[1,8,128]{2,1,0:T(8,128)S(1)} %get-tuple-element.115), channel_id=1, source_target_pairs={{16,0},{32,16},{48,32},{64,48},{80,64},{96,80},{112,96},{128,112},... | collective-permute-start | bytes 12296 | tf_op jit(solution)/shard_map/ppermute | solution.py:22
  97.0 8.7 %collective-permute-start.13 = (f32[1,8,128]{2,1,0:T(8,128)S(1)}, f32[1,8,128]{2,1,0:T(8,128)S(1)}, u32[]{:S(2)}, u32[]{:S(2)}) collective-permute-start(f32[1,8,128]{2,1,0:T(8,128)S(1)} %get-tuple-element.114), channel_id=1, source_target_pairs={{0,16},{16,32},{32,48},{48,64},{64,80},{80,96},{96,112},{112,128},... | collective-permute-start | bytes 12296 | tf_op jit(solution)/shard_map/ppermute | solution.py:21
  105.7 6.1 collective-permute-start.14
  106.9 5.6 collective-permute-start.15
  112.7 123.6 %copy-start.10 = (f32[4,8,128]{2,1,0:T(8,128)}, f32[4,8,128]{2,1,0:T(8,128)S(1)}, u32[]{:S(2)}) copy-start(f32[4,8,128]{2,1,0:T(8,128)S(1)} %get-tuple-element.49) | copy-start | bytes 49156
  112.7 10.9 %collective-permute-start.16 = (f32[1,8,128]{2,1,0:T(8,128)S(1)}, f32[1,8,128]{2,1,0:T(8,128)S(1)}, u32[]{:S(2)}, u32[]{:S(2)}) collective-permute-start(f32[1,8,128]{2,1,0:T(8,128)S(1)} %get-tuple-element.113), channel_id=1, source_target_pairs={{16,0},{32,16},{48,32},{64,48},{80,64},{96,80},{112,96},{128,112},... | collective-permute-start | bytes 12296 | tf_op jit(solution)/shard_map/ppermute | solution.py:22
  114.7 9.7 %collective-permute-start.17 = (f32[1,8,128]{2,1,0:T(8,128)S(1)}, f32[1,8,128]{2,1,0:T(8,128)S(1)}, u32[]{:S(2)}, u32[]{:S(2)}) collective-permute-start(f32[1,8,128]{2,1,0:T(8,128)S(1)} %get-tuple-element.112), channel_id=1, source_target_pairs={{0,16},{16,32},{32,48},{48,64},{64,80},{80,96},{96,112},{112,128},... | collective-permute-start | bytes 12296 | tf_op jit(solution)/shard_map/ppermute | solution.py:21
  124.4 5.8 collective-permute-start.18
  125.7 5.3 collective-permute-start.19
  131.1 105.1 %copy-start.11 = (f32[4,8,128]{2,1,0:T(8,128)}, f32[4,8,128]{2,1,0:T(8,128)S(1)}, u32[]{:S(2)}) copy-start(f32[4,8,128]{2,1,0:T(8,128)S(1)} %get-tuple-element.47) | copy-start | bytes 49156
  131.2 10.9 %collective-permute-start.20 = (f32[1,8,128]{2,1,0:T(8,128)S(1)}, f32[1,8,128]{2,1,0:T(8,128)S(1)}, u32[]{:S(2)}, u32[]{:S(2)}) collective-permute-start(f32[1,8,128]{2,1,0:T(8,128)S(1)} %get-tuple-element.111), channel_id=1, source_target_pairs={{16,0},{32,16},{48,32},{64,48},{80,64},{96,80},{112,96},{128,112},... | collective-permute-start | bytes 12296 | tf_op jit(solution)/shard_map/ppermute | solution.py:22
  133.1 9.7 %collective-permute-start.21 = (f32[1,8,128]{2,1,0:T(8,128)S(1)}, f32[1,8,128]{2,1,0:T(8,128)S(1)}, u32[]{:S(2)}, u32[]{:S(2)}) collective-permute-start(f32[1,8,128]{2,1,0:T(8,128)S(1)} %get-tuple-element.110), channel_id=1, source_target_pairs={{0,16},{16,32},{32,48},{48,64},{64,80},{80,96},{96,112},{112,128},... | collective-permute-start | bytes 12296 | tf_op jit(solution)/shard_map/ppermute | solution.py:21
  142.8 6.5 %collective-permute-start.22 = (f32[6,1,128]{2,1,0:T(1,128)S(1)}, f32[6,1,128]{2,1,0:T(1,128)S(1)}, u32[]{:S(2)}, u32[]{:S(2)}) collective-permute-start(f32[6,1,128]{2,1,0:T(1,128)S(1)} %get-tuple-element.96), channel_id=1, source_target_pairs={{1,0},{2,1},{3,2},{4,3},{5,4},{6,5},{7,6},{8,7},{9,8},{10,9},{11,1... | collective-permute-start | bytes 9224 | tf_op jit(solution)/shard_map/ppermute | solution.py:22
  144.1 6.0 collective-permute-start.23
  151.2 10.9 %collective-permute-start.24 = (bf16[1,10,128]{2,1,0:T(8,128)(2,1)S(1)}, bf16[1,10,128]{2,1,0:T(8,128)(2,1)S(1)}, u32[]{:S(2)}, u32[]{:S(2)}) collective-permute-start(bf16[1,10,128]{2,1,0:T(8,128)(2,1)S(1)} %get-tuple-element.88), channel_id=1, source_target_pairs={{0,16},{16,32},{32,48},{48,64},{64,80},{80,96},{96,112},{112,128},... | collective-permute-start | bytes 7688 | tf_op jit(solution)/shard_map/ppermute | solution.py:34
  160.2 8.8 %collective-permute-start.25 = (bf16[1,10,128]{2,1,0:T(8,128)(2,1)S(1)}, bf16[1,10,128]{2,1,0:T(8,128)(2,1)S(1)}, u32[]{:S(2)}, u32[]{:S(2)}) collective-permute-start(bf16[1,10,128]{2,1,0:T(8,128)(2,1)S(1)} %get-tuple-element.89), channel_id=1, source_target_pairs={{16,0},{32,16},{48,32},{64,48},{80,64},{96,80},{112,96},{128,112},... | collective-permute-start | bytes 7688 | tf_op jit(solution)/shard_map/ppermute | solution.py:34
  169.1 7.1 %collective-permute-start.26 = (bf16[4,1,128]{2,1,0:T(2,128)(2,1)S(1)}, bf16[4,1,128]{2,1,0:T(2,128)(2,1)S(1)}, u32[]{:S(2)}, u32[]{:S(2)}) collective-permute-start(bf16[4,1,128]{2,1,0:T(2,128)(2,1)S(1)} %get-tuple-element.107), channel_id=1, source_target_pairs={{0,1},{1,2},{2,3},{3,4},{4,5},{5,6},{6,7},{7,8},{8,9},{9,10},{10,1... | collective-permute-start | bytes 3080 | tf_op jit(solution)/shard_map/ppermute | solution.py:34
  174.9 7.0 %collective-permute-start.27 = (bf16[4,1,128]{2,1,0:T(2,128)(2,1)S(1)}, bf16[4,1,128]{2,1,0:T(2,128)(2,1)S(1)}, u32[]{:S(2)}, u32[]{:S(2)}) collective-permute-start(bf16[4,1,128]{2,1,0:T(2,128)(2,1)S(1)} %get-tuple-element.108), channel_id=1, source_target_pairs={{1,0},{2,1},{3,2},{4,3},{5,4},{6,5},{7,6},{8,7},{9,8},{10,9},{11,1... | collective-permute-start | bytes 3080 | tf_op jit(solution)/shard_map/ppermute | solution.py:34
  182.7 5.0 collective-permute-start.28
  185.8 8.8 %collective-permute-start.29 = (bf16[1,10,128]{2,1,0:T(8,128)(2,1)S(1)}, bf16[1,10,128]{2,1,0:T(8,128)(2,1)S(1)}, u32[]{:S(2)}, u32[]{:S(2)}) collective-permute-start(bf16[1,10,128]{2,1,0:T(8,128)(2,1)S(1)} %get-tuple-element.87), channel_id=1, source_target_pairs={{16,0},{32,16},{48,32},{64,48},{80,64},{96,80},{112,96},{128,112},... | collective-permute-start | bytes 7688 | tf_op jit(solution)/shard_map/ppermute | solution.py:34
  194.7 7.3 %collective-permute-start.30 = (bf16[4,1,128]{2,1,0:T(2,128)(2,1)S(1)}, bf16[4,1,128]{2,1,0:T(2,128)(2,1)S(1)}, u32[]{:S(2)}, u32[]{:S(2)}) collective-permute-start(bf16[4,1,128]{2,1,0:T(2,128)(2,1)S(1)} %get-tuple-element.105), channel_id=1, source_target_pairs={{0,1},{1,2},{2,3},{3,4},{4,5},{5,6},{6,7},{7,8},{8,9},{9,10},{10,1... | collective-permute-start | bytes 3080 | tf_op jit(solution)/shard_map/ppermute | solution.py:34
  200.7 7.0 %collective-permute-start.31 = (bf16[4,1,128]{2,1,0:T(2,128)(2,1)S(1)}, bf16[4,1,128]{2,1,0:T(2,128)(2,1)S(1)}, u32[]{:S(2)}, u32[]{:S(2)}) collective-permute-start(bf16[4,1,128]{2,1,0:T(2,128)(2,1)S(1)} %get-tuple-element.106), channel_id=1, source_target_pairs={{1,0},{2,1},{3,2},{4,3},{5,4},{6,5},{7,6},{8,7},{9,8},{10,9},{11,1... | collective-permute-start | bytes 3080 | tf_op jit(solution)/shard_map/ppermute | solution.py:34
  208.5 5.0 collective-permute-start.32
  211.6 8.8 %collective-permute-start.33 = (bf16[1,10,128]{2,1,0:T(8,128)(2,1)S(1)}, bf16[1,10,128]{2,1,0:T(8,128)(2,1)S(1)}, u32[]{:S(2)}, u32[]{:S(2)}) collective-permute-start(bf16[1,10,128]{2,1,0:T(8,128)(2,1)S(1)} %get-tuple-element.85), channel_id=1, source_target_pairs={{16,0},{32,16},{48,32},{64,48},{80,64},{96,80},{112,96},{128,112},... | collective-permute-start | bytes 7688 | tf_op jit(solution)/shard_map/ppermute | solution.py:34
  221.7 24.3 %collective-permute-start.34 = (bf16[4,1,128]{2,1,0:T(2,128)(2,1)}, bf16[4,1,128]{2,1,0:T(2,128)(2,1)}, u32[]{:S(2)}, u32[]{:S(2)}) collective-permute-start(bf16[4,1,128]{2,1,0:T(2,128)(2,1)} %get-tuple-element.103), channel_id=1, source_target_pairs={{0,1},{1,2},{2,3},{3,4},{4,5},{5,6},{6,7},{7,8},{8,9},{9,10},{10,1... | collective-permute-start | bytes 3080 | tf_op jit(solution)/shard_map/ppermute | solution.py:34
  228.1 18.0 %collective-permute-start.35 = (bf16[4,1,128]{2,1,0:T(2,128)(2,1)}, bf16[4,1,128]{2,1,0:T(2,128)(2,1)}, u32[]{:S(2)}, u32[]{:S(2)}) collective-permute-start(bf16[4,1,128]{2,1,0:T(2,128)(2,1)} %get-tuple-element.104), channel_id=1, source_target_pairs={{1,0},{2,1},{3,2},{4,3},{5,4},{6,5},{7,6},{8,7},{9,8},{10,9},{11,1... | collective-permute-start | bytes 3080 | tf_op jit(solution)/shard_map/ppermute | solution.py:34
  273.8 34.4 %collective-permute-start.36 = (bf16[16,1,10,128]{3,0,2,1:T(8,128)(2,1)S(1)}, bf16[16,1,10,128]{3,0,2,1:T(8,128)(2,1)S(1)}, u32[]{:S(2)}, u32[]{:S(2)}) collective-permute-start(bf16[16,1,10,128]{3,0,2,1:T(8,128)(2,1)S(1)} %get-tuple-element.54), channel_id=1, source_target_pairs={{0,16},{16,32},{32,48},{48,64},{64,80},{80,96},{96,112},{112,128},... | collective-permute-start | bytes 122888 | tf_op jit(solution)/shard_map/ppermute | solution.py:34
  276.1 32.1 %collective-permute-start.37 = (bf16[16,1,10,128]{3,0,2,1:T(8,128)(2,1)S(1)}, bf16[16,1,10,128]{3,0,2,1:T(8,128)(2,1)S(1)}, u32[]{:S(2)}, u32[]{:S(2)}) collective-permute-start(bf16[16,1,10,128]{3,0,2,1:T(8,128)(2,1)S(1)} %get-tuple-element.55), channel_id=1, source_target_pairs={{16,0},{32,16},{48,32},{64,48},{80,64},{96,80},{112,96},{128,112},... | collective-permute-start | bytes 122888 | tf_op jit(solution)/shard_map/ppermute | solution.py:34
  308.4 5.8 collective-permute-start.38
  312.5 4.9 collective-permute-start.39
  538.4 107.4 %copy-start.1 = (bf16[16,16,3,3,3]{1,0,4,3,2:T(8,128)(2,1)S(1)}, bf16[16,16,3,3,3]{1,0,4,3,2:T(8,128)(2,1)}, u32[]{:S(2)}) copy-start(bf16[16,16,3,3,3]{1,0,4,3,2:T(8,128)(2,1)} %param.10) | copy-start | bytes 41476
  608.7 25.8 %collective-permute-start.40 = (bf16[16,1,10,128]{3,0,2,1:T(8,128)(2,1)S(1)}, bf16[16,1,10,128]{3,0,2,1:T(8,128)(2,1)S(1)}, u32[]{:S(2)}, u32[]{:S(2)}) collective-permute-start(bf16[16,1,10,128]{3,0,2,1:T(8,128)(2,1)S(1)} %get-tuple-element.52), channel_id=1, source_target_pairs={{0,16},{16,32},{32,48},{48,64},{64,80},{80,96},{96,112},{112,128},... | collective-permute-start | bytes 122888 | tf_op jit(solution)/shard_map/ppermute | solution.py:34
  629.9 9.2 %collective-permute-start.41 = (bf16[16,1,10,128]{3,0,2,1:T(8,128)(2,1)S(1)}, bf16[16,1,10,128]{3,0,2,1:T(8,128)(2,1)S(1)}, u32[]{:S(2)}, u32[]{:S(2)}) collective-permute-start(bf16[16,1,10,128]{3,0,2,1:T(8,128)(2,1)S(1)} %get-tuple-element.53), channel_id=1, source_target_pairs={{16,0},{32,16},{48,32},{64,48},{80,64},{96,80},{112,96},{128,112},... | collective-permute-start | bytes 122888 | tf_op jit(solution)/shard_map/ppermute | solution.py:34
  639.3 4.7 collective-permute-start.42
  640.6 4.5 collective-permute-start.43
  (22 other events, 446.7 us)
